TPU v7x, 256 devices: a whole 4x4x8 slice. The times are simulated.
256 devices in a mesh: rows: 64 (over z_hi, y, x, core), ch: 4 (over z_lo).
Axes of the slice: x: 4, y: 4, z: 8 (z_hi: 2, z_lo: 4; z = z_hi * 4 + z_lo), core: 2. Of those that a mesh axis runs over, the one named last changes fastest.
Arguments:
- pixels: bfloat16 [256, 96, 2048], P('rows', 'ch'), may hold values from -6 to 6
- depth_weight: float32 [96, 9], P('ch'), may hold values from -2 to 2
- mix_weight: bfloat16 [96, 96], replicated, may hold values from -0.625 to 0.625
- spectral_real: bfloat16 [256, 96, 1024], P(None, 'ch', 'rows'), may hold values from -4 to 4
- spectral_imag: bfloat16 [256, 96, 1024], P(None, 'ch', 'rows'), may hold values from -4 to 4
- query_weight: bfloat16 [96, 128], P('ch'), may hold values from -0.625 to 0.625
- key_weight: bfloat16 [96, 128], P('ch'), may hold values from -0.625 to 0.625
- query_pixels: int32 [4096], P('rows'), may hold values from 0 to 8191
- key_pixels: int32 [16384], P('rows'), may hold values from 0 to 8191
- positives: int32 [4096], P('rows'), may hold values from 0 to 16383
Outputs:
- encoded: bfloat16 [256, 96, 2048], P('rows', 'ch')
- losses: float32 [4096], P(('rows', 'ch'))
Inputs may be any that keep to these rules, and one draw needn't show every extreme that they name: `query_pixels`: each entry is r * 2048 + x for a pixel at row r and column x of the query's own slab of 4 rows. `key_pixels`: each entry is r * 2048 + x for a pixel at row r and column x of the key's own slab of 4 rows. `positives`: the number of the positive key among all 16384 keys, numbered slab by slab in the order of key_pixels.
All inputs are finite; a program needn't handle non-finite values.
Results may differ from a plain program's by a relative error of at most 0.0065.
Values may be sent and summed in bfloat16 or wider, within the bound.
A program may use at most 64 MiB of HBM per device.

v0:
```python
import jax
import jax.numpy as jnp
from jax import lax
from jax.sharding import PartitionSpec as P

DILATION = 2
score_scale = 10.0
exact = lax.Precision.HIGHEST


def extended(cells, sides, width):
    for axis, dim in sides:
        count = lax.axis_size(axis)
        ends = count - 1
        head = lax.slice_in_dim(cells, 0, width, axis=dim)
        tail = lax.slice_in_dim(cells, cells.shape[dim] - width, cells.shape[dim], axis=dim)
        cells = jnp.concatenate(
            [
                lax.ppermute(tail, axis, [(i, (i + 1) % count) for i in range(ends)]),
                cells,
                lax.ppermute(head, axis, [((i + 1) % count, i) for i in range(ends)]),
            ],
            axis=dim,
        )
    return cells


def unit_rows(values):
    return values * lax.rsqrt(jnp.sum(values * values, axis=1, keepdims=True) + 1e-06)


def angle_table(left_len, right_len, length, direction):
    left_index = lax.broadcasted_iota(jnp.int32, (left_len, right_len), 0)
    right_index = lax.broadcasted_iota(jnp.int32, (left_len, right_len), 1)
    phase_turns = left_index * right_index % length
    angles = phase_turns.astype(jnp.float32) * (direction * 2.0 * jnp.pi / length)
    return (jnp.cos(angles), jnp.sin(angles))


def transform_last(real_part, imag_part, direction, real_only, lower_half):
    length = real_part.shape[-1]
    first_len = 1 << (length.bit_length() - 1) // 2
    second = length // first_len
    kept = second // 2 if lower_half else second
    leading = real_part.shape[:-1]
    cos_first, sin_first = angle_table(first_len, first_len, first_len, direction)
    cos_twist, sin_twist = angle_table(first_len, second, length, direction)
    cos_second, sin_second = angle_table(second, second, second, direction)
    cos_second = cos_second[:, :kept]
    sin_second = sin_second[:, :kept]

    def over_first(matrix, values):
        return jnp.einsum("ka,...ab->...kb", matrix, values, precision=exact)

    def over_second(values, matrix):
        return jnp.einsum("...kb,bm->...km", values, matrix, precision=exact)

    real_grid = real_part.reshape(leading + (first_len, second))
    if imag_part is None:
        segment_real = over_first(cos_first, real_grid)
        segment_imag = over_first(sin_first, real_grid)
    else:
        imag_grid = imag_part.reshape(leading + (first_len, second))
        segment_real = over_first(cos_first, real_grid) - over_first(sin_first, imag_grid)
        segment_imag = over_first(sin_first, real_grid) + over_first(cos_first, imag_grid)
    twisted_real = segment_real * cos_twist - segment_imag * sin_twist
    twisted_imag = segment_real * sin_twist + segment_imag * cos_twist
    result_real = over_second(twisted_real, cos_second) - over_second(twisted_imag, sin_second)
    result_real = jnp.swapaxes(result_real, -1, -2).reshape(leading + (kept * first_len,))
    if real_only:
        return result_real
    result_imag = over_second(twisted_real, sin_second) + over_second(twisted_imag, cos_second)
    result_imag = jnp.swapaxes(result_imag, -1, -2).reshape(leading + (kept * first_len,))
    return (result_real, result_imag)


def transform_first(real_part, imag_part, direction):
    moved_real = jnp.moveaxis(real_part, 0, -1)
    moved_imag = jnp.moveaxis(imag_part, 0, -1)
    result_real, result_imag = transform_last(moved_real, moved_imag, direction, False, False)
    return (jnp.moveaxis(result_real, -1, 0), jnp.moveaxis(result_imag, -1, 0))


def score_fold(query_unit, targets, key_number):

    def add_block(carried, shard_piece, offset):
        scores = (
            jnp.einsum("qd,kd->qk", query_unit, shard_piece, preferred_element_type=jnp.float32)
            * score_scale
        )
        numbers = key_number(lax.broadcasted_iota(jnp.int32, (1, shard_piece.shape[0]), 1))
        exp_sums = jnp.sum(jnp.exp(scores), axis=1)
        picked = jnp.sum(jnp.where(targets[:, None] == numbers, scores, 0.0), axis=1)
        return (exp_sums, picked)

    return add_block


def same_number(gathered):
    return gathered


def body(
    pixels,
    depth_weight,
    mix_weight,
    spectral_real,
    spectral_imag,
    query_weight,
    key_weight,
    query_pixels,
    key_pixels,
    positives,
):
    slab_rows, groups, columns = pixels.shape
    half_cols = columns // 2
    channel = lax.axis_index("ch")
    group_count = lax.axis_size("ch")
    padded = extended(pixels, (("rows", 0),), DILATION)
    padded = jnp.pad(padded, ((0, 0), (0, 0), (DILATION, DILATION)))
    summed = pixels.astype(jnp.float32)
    for tap_row in range(3):
        for tap_col in range(3):
            shifted = padded[
                tap_row * DILATION : tap_row * DILATION + slab_rows,
                :,
                tap_col * DILATION : tap_col * DILATION + columns,
            ]
            summed = summed + depth_weight[:, 3 * tap_row + tap_col][
                None, :, None
            ] * shifted.astype(jnp.float32)
    conv_out = summed.astype(jnp.bfloat16)
    local_columns = lax.dynamic_slice_in_dim(mix_weight, channel * groups, groups, 1)
    mixture = jnp.einsum(
        "rcw,cd->rdw",
        lax.all_gather(conv_out, "ch", axis=1, tiled=True),
        local_columns,
        preferred_element_type=jnp.float32,
    )
    hidden = jax.nn.gelu(mixture).astype(jnp.bfloat16)
    spectrum_real, spectrum_imag = transform_last(
        hidden.astype(jnp.float32), None, -1.0, False, True
    )
    wire = jnp.stack([spectrum_real, spectrum_imag]).astype(jnp.bfloat16)
    columns_both = lax.all_to_all(wire, "rows", split_axis=3, concat_axis=1, tiled=True)
    column_real, column_imag = (columns_both[0], columns_both[1])
    full_real, full_imag = transform_first(
        column_real.astype(jnp.float32), column_imag.astype(jnp.float32), -1.0
    )
    kernel_real = spectral_real.astype(jnp.float32)
    kernel_imag = spectral_imag.astype(jnp.float32)
    product_real = full_real * kernel_real - full_imag * kernel_imag
    product_imag = full_real * kernel_imag + full_imag * kernel_real
    back_real, back_imag = transform_first(product_real, product_imag, 1.0)
    height = column_real.shape[0]
    back_real = (back_real * (1.0 / height)).astype(jnp.bfloat16)
    back_imag = (back_imag * (1.0 / height)).astype(jnp.bfloat16)
    rows_both = lax.all_to_all(
        jnp.stack([back_real, back_imag]), "rows", split_axis=1, concat_axis=3, tiled=True
    )
    row_real, row_imag = (rows_both[0], rows_both[1])
    doubling = jnp.where(lax.broadcasted_iota(jnp.int32, (1, 1, half_cols), 2) == 0, 1.0, 2.0)
    wide_real = jnp.pad(
        row_real.astype(jnp.float32) * doubling, ((0, 0), (0, 0), (0, columns - half_cols))
    )
    wide_imag = jnp.pad(
        row_imag.astype(jnp.float32) * doubling, ((0, 0), (0, 0), (0, columns - half_cols))
    )
    spatial = transform_last(wide_real, wide_imag, 1.0, True, False) * (1.0 / columns)
    encoded = (hidden.astype(jnp.float32) + spatial).astype(jnp.bfloat16)
    key_count = key_pixels.shape[0]
    query_count = query_pixels.shape[0]
    quarter = query_count // group_count
    slab = lax.axis_index("rows")
    weights_all = lax.all_gather(
        jnp.concatenate([key_weight, query_weight], axis=1), "ch", axis=0, tiled=True
    )
    sampled = jnp.concatenate([key_pixels, query_pixels])
    features = encoded[sampled // columns, :, sampled % columns]
    features = lax.all_gather(features, "ch", axis=1, tiled=True)
    key_dim = key_weight.shape[1]
    key_unit = unit_rows(
        jnp.dot(features[:key_count], weights_all[:, :key_dim], preferred_element_type=jnp.float32)
    ).astype(jnp.bfloat16)
    own_queries = lax.dynamic_slice_in_dim(features, key_count + channel * quarter, quarter, 0)
    query_unit = unit_rows(
        jnp.dot(own_queries, weights_all[:, key_dim:], preferred_element_type=jnp.float32)
    ).astype(jnp.bfloat16)
    targets = lax.dynamic_slice_in_dim(positives, channel * quarter, quarter, 0)
    coded = jnp.concatenate([targets // 128, targets % 128]).astype(jnp.bfloat16)
    coded = jnp.pad(coded, (0, key_dim - 2 * quarter))[None, :]
    packet = jnp.concatenate([query_unit, coded], axis=0)
    gathered = lax.all_gather(packet[None], "rows", axis=0, tiled=True)
    all_queries = gathered[:, :quarter, :].reshape(-1, key_dim)
    coded_all = gathered[:, quarter, :].astype(jnp.int32)
    all_targets = (coded_all[:, :quarter] * 128 + coded_all[:, quarter : 2 * quarter]).reshape(-1)
    scores = (
        jnp.einsum("qd,kd->qk", all_queries, key_unit, preferred_element_type=jnp.float32)
        * score_scale
    )
    numbers = slab * key_count + lax.broadcasted_iota(jnp.int32, (1, key_count), 1)
    exp_sums = jnp.sum(jnp.exp(scores), axis=1)
    picked = jnp.sum(jnp.where(all_targets[:, None] == numbers, scores, 0.0), axis=1)
    reduced = lax.psum_scatter(
        jnp.stack([exp_sums, picked], axis=1), "rows", scatter_dimension=0, tiled=True
    )
    losses = jnp.log(reduced[:, 0]) - reduced[:, 1]
    return (encoded, losses)


def solution(mesh):
    placed = (
        P("rows", "ch", None),
        P("ch", None),
        P(),
        P(None, "ch", "rows"),
        P(None, "ch", "rows"),
        P("ch", None),
        P("ch", None),
        P("rows"),
        P("rows"),
        P("rows"),
    )
    return jax.shard_map(
        body,
        mesh=mesh,
        in_specs=placed,
        out_specs=(P("rows", "ch", None), P(("rows", "ch"))),
        check_vma=False,
    )
```

profile of v0, /device:TPU:32, one launch (start us, length us, event | category | flops | bytes accessed | tf_op | source)
XLA Modules:
  0.0 866.5 jit_solution(4636469104525805419)
XLA Ops:
  17.9 56.4 %all-gather.4.cloned.1.call-done = bf16[4,96,2048]{2,1,0:T(8,128)(2,1)} async-done(((bf16[4,24,2048]{2,1,0:T(8,128)(2,1)}), bf16[4,96,2048]{2,1,0:T(8,128)(2,1)}) %all-gather.4.cloned.1.call-update) | async-done | bytes 1572880 | tf_op jit(solution)/shard_map/all_gather | solution.py:136
  92.4 3.8 fusion.45
  100.2 3.6 reshape.434
  103.8 11.1 %all-to-all-start = ((bf16[64,2,1536]{2,1,0:T(2,128)(2,1)}), bf16[64,2,1536]{2,1,0:T(2,128)(2,1)S(1)}, u32[]{:S(2)}, u32[]{:S(2)}) async-start(bf16[64,2,1536]{2,1,0:T(2,128)(2,1)} %reshape.434), calls=%async_computation | async-start | bytes 786432 | tf_op jit(solution)/shard_map/all_to_all | solution.py:145
  115.0 16.3 %all_gather.14 = bf16[96,256]{1,0:T(8,128)(2,1)S(1)} all-gather(bf16[24,256]{1,0:T(8,128)(2,1)S(1)} %pad_maximum_fusion.4), channel_id=1, replica_groups=mesh['rows'=64,'ch'=4] {'ch'}, dimensions={0}, use_global_device_ids=true | all-gather | bytes 61440 | tf_op jit(solution)/shard_map/all_gather | solution.py:175
  132.3 3.9 reshape.435
  136.2 5.5 copy.239
  144.5 3.6 copy.177
  153.3 4.1 copy.181
  166.6 3.8 subtract_bitcast_fusion
  170.4 4.0 add_bitcast_fusion
  174.4 3.8 copy.194
  180.3 3.8 copy.191
  202.8 3.8 copy.197
  206.7 3.8 convolution_subtract_fusion
  220.7 3.6 fusion.39
  224.3 3.9 copy.205
  237.1 3.6 reshape.436
  240.6 11.9 %all-to-all-start.1 = ((bf16[64,2,1536]{2,1,0:T(2,128)(2,1)}), bf16[64,2,1536]{2,1,0:T(2,128)(2,1)S(1)}, u32[]{:S(2)}, u32[]{:S(2)}) async-start(bf16[64,2,1536]{2,1,0:T(2,128)(2,1)} %reshape.436), calls=%async_computation.1 | async-start | bytes 786432 | tf_op jit(solution)/shard_map/all_to_all | solution.py:158
  252.9 17.5 %all-to-all-done.1 = bf16[64,2,1536]{2,1,0:T(2,128)(2,1)S(1)} async-done(((bf16[64,2,1536]{2,1,0:T(2,128)(2,1)}), bf16[64,2,1536]{2,1,0:T(2,128)(2,1)S(1)}, u32[]{:S(2)}, u32[]{:S(2)}) %all-to-all-start.1) | async-done | bytes 393248 | tf_op jit(solution)/shard_map/all_to_all | solution.py:158
  314.0 4.9 gather_fusion
  319.0 12.0 %all_gather.13 = bf16[320,96]{0,1:T(8,128)(2,1)S(1)} all-gather(bf16[320,24]{0,1:T(8,128)(2,1)S(1)} %copy.218), channel_id=1, replica_groups=mesh['rows'=64,'ch'=4] {'ch'}, dimensions={1}, use_global_device_ids=true | all-gather | bytes 76800 | tf_op jit(solution)/shard_map/all_gather | solution.py:180
  331.7 110.5 %all-gather.1 = bf16[64,17,128]{2,1,0:T(8,128)(2,1)S(1)} all-gather(bf16[1,17,128]{2,1,0:T(8,128)(2,1)S(1)} %maximum_bitcast_fusion), channel_id=2, replica_groups=mesh['rows'=64,'ch'=4] {'rows'}, dimensions={0}, use_global_device_ids=true | all-gather | bytes 282880 | tf_op jit(solution)/shard_map/all_gather | solution.py:193
  443.9 414.0 %reduce-scatter.4.cloned.1.call-done = f32[16,2]{1,0:T(8,128)} async-done(((f32[1024,2]{1,0:T(8,128)}), f32[16,2]{1,0:T(8,128)}) %reduce-scatter.4.cloned.1.call-update) | async-done | bytes 144
  (132 shorter events, 138.5 us)
Async XLA Ops:
  7.2 67.2 %copy-start = (bf16[96,96]{1,0:T(8,128)(2,1)S(1)}, bf16[96,96]{1,0:T(8,128)(2,1)}, u32[]{:S(2)}) copy-start(bf16[96,96]{1,0:T(8,128)(2,1)} %param.12) | copy-start | bytes 55300
  7.2 8.8 %copy-start.5 = (bf16[4,24,2048]{2,1,0:T(8,128)(2,1)S(1)}, bf16[4,24,2048]{2,1,0:T(8,128)(2,1)}, u32[]{:S(2)}) copy-start(bf16[4,24,2048]{2,1,0:T(8,128)(2,1)} %param.10) | copy-start | bytes 1179652
  7.2 67.1 %all-gather.4.cloned.1.call-start = ((), (), s32[]{:S(2)}) async-start(), calls=%async_computation.3 | async-start | bytes 1966080 | tf_op jit(solution)/shard_map/all_gather | solution.py:136
  8.3 4.0 collective-permute-start
  10.1 4.6 collective-permute-start.1
  76.3 0.8 copy-start.7
  77.9 0.9 copy-start.4
  100.2 14.7 %copy-start.12 = (s32[256]{0:T(256)S(1)}, s32[256]{0:T(256)}, u32[]{:S(2)}) copy-start(s32[256]{0:T(256)} %param.18) | copy-start | bytes 3076
  100.2 14.7 %copy-start.13 = (s32[64]{0:T(128)S(1)}, s32[64]{0:T(128)}, u32[]{:S(2)}) copy-start(s32[64]{0:T(128)} %param.17) | copy-start | bytes 772
  100.2 14.8 %copy-start.10 = (bf16[24,128]{1,0:T(8,128)(2,1)S(1)}, bf16[24,128]{1,0:T(8,128)(2,1)}, u32[]{:S(2)}) copy-start(bf16[24,128]{1,0:T(8,128)(2,1)} %param.15) | copy-start | bytes 18436
  100.2 14.7 %copy-start.11 = (bf16[24,128]{1,0:T(8,128)(2,1)S(1)}, bf16[24,128]{1,0:T(8,128)(2,1)}, u32[]{:S(2)}) copy-start(bf16[24,128]{1,0:T(8,128)(2,1)} %param.16) | copy-start | bytes 18436
  103.8 28.5 %all-to-all-start = ((bf16[64,2,1536]{2,1,0:T(2,128)(2,1)}), bf16[64,2,1536]{2,1,0:T(2,128)(2,1)S(1)}, u32[]{:S(2)}, u32[]{:S(2)}) async-start(bf16[64,2,1536]{2,1,0:T(2,128)(2,1)} %reshape.434), calls=%async_computation | async-start | bytes 786432 | tf_op jit(solution)/shard_map/all_to_all | solution.py:145
  157.4 2.0 copy-start.3
  184.1 2.1 copy-start.9
  206.6 3.8 copy-start.2
  237.0 15.5 %copy-start.14 = (s32[64]{0:T(128)S(1)}, s32[64]{0:T(128)}, u32[]{:S(2)}) copy-start(s32[64]{0:T(128)} %param.19) | copy-start | bytes 772
  240.6 29.8 %all-to-all-start.1 = ((bf16[64,2,1536]{2,1,0:T(2,128)(2,1)}), bf16[64,2,1536]{2,1,0:T(2,128)(2,1)S(1)}, u32[]{:S(2)}, u32[]{:S(2)}) async-start(bf16[64,2,1536]{2,1,0:T(2,128)(2,1)} %reshape.436), calls=%async_computation.1 | async-start | bytes 786432 | tf_op jit(solution)/shard_map/all_to_all | solution.py:158
  252.5 605.5 %reduce-scatter.4.cloned.1.call-start = ((), (), s32[]{:S(2)}) async-start(), calls=%async_computation.4 | async-start | bytes 532480
  293.6 1.5 copy-start.8
  313.0 129.2 %copy-start.6 = (bf16[4,24,2048]{2,1,0:T(8,128)(2,1)}, bf16[4,24,2048]{2,1,0:T(8,128)(2,1)S(1)}, u32[]{:S(2)}) copy-start(bf16[4,24,2048]{2,1,0:T(8,128)(2,1)S(1)} %add_convert_fusion.1) | copy-start | bytes 1179652
  331.6 527.9 %copy-start.1 = (bf16[96,96]{1,0:T(8,128)(2,1)S(1)}, bf16[96,96]{1,0:T(8,128)(2,1)}, u32[]{:S(2)}) copy-start(bf16[96,96]{1,0:T(8,128)(2,1)} %param.12) | copy-start | bytes 55300
Sparse Core Ops, SparseCore 0:
  17.9 56.3 all-gather.3
  444.1 413.8 reduce-scatter.3
where the time goes:
time: 876 us; the launch traced here: 867 us
  waiting for transfers between devices  491 us (56%)
  blocking collectives  139 us (16%)
  local copies, waits for them, and re-layouts  109 us (12%)
  matrix products  75.7 us (9%)
  starting transfers between devices  26.1 us (3%)
  between operations  14.9 us (2%)
  other arithmetic  10.4 us (1%)
    unnamed x3, waiting for transfers between devices  414 us
    all_gather x1, blocking collectives, body(): gathered = lax.all_gather(packet[None], 'rows', axis=0, tiled=True)  110 us
    all_gather x1, waiting for transfers between devices, body(): lax.all_gather(conv_out, 'ch', axis=1, tiled=True)  56.4 us
    dot_general x14, matrix products, over_second(): return jnp.einsum('...kb,bm->...km', values, matrix, precision=exact)  38.5 us
    dot_general x14, matrix products, over_first(): return jnp.einsum('ka,...ab->...kb', matrix, values, precision=exact)  34.2 us
    all_to_all x1, waiting for transfers between devices, body(): lax.all_to_all(jnp.stack([back_real, back_imag]), 'rows', split_axis=1, c...  17.5 us
  transfers between devices with their start and end apart: 6, of which 5 were waited for; matrix products, arithmetic and copies ran while one was open for 0% of the time, Pallas kernels for 0%

commit v1 on v0

--- a/solution.py
+++ b/solution.py
@@ -190,7 +190,9 @@
     coded = jnp.concatenate([targets // 128, targets % 128]).astype(jnp.bfloat16)
     coded = jnp.pad(coded, (0, key_dim - 2 * quarter))[None, :]
     packet = jnp.concatenate([query_unit, coded], axis=0)
-    gathered = lax.all_gather(packet[None], "rows", axis=0, tiled=True)
+    gathered = jnp.concatenate(
+        lax.all_to_all(jnp.stack([packet[None]] * lax.axis_size("rows")), "rows", 0, 0), axis=0
+    )
     all_queries = gathered[:, :quarter, :].reshape(-1, key_dim)
     coded_all = gathered[:, quarter, :].astype(jnp.int32)
     all_targets = (coded_all[:, :quarter] * 128 + coded_all[:, quarter : 2 * quarter]).reshape(-1)

time: 876 us -> 787 us (0.90)
  blocking collectives: 139 us -> 28.6 us
  waiting for transfers between devices: 491 us -> 506 us
    all_gather x1 -> x0, blocking collectives: 110 us -> none  [body(): gathered = lax.all_gather(packet[None], 'rows', axis=0, tiled=True)]
    all_to_all x0 -> x1, waiting for transfers between devices: none -> 17.8 us  [body(): lax.all_to_all(jnp.stack([packet[None]] * lax.axis_size('rows')), 'rows',...]
    all_to_all x1, waiting for transfers between devices: 0.89 us -> 17.4 us  [body(): lax.all_to_all(wire, 'rows', split_axis=3, concat_axis=1, tiled=True)]
    all_to_all x1, waiting for transfers between devices: 17.5 us -> 1.53 us  [body(): lax.all_to_all(jnp.stack([back_real, back_imag]), 'rows', split_axis=1, c...]
    all_to_all x0 -> x1, starting transfers between devices: none -> 12.8 us  [body(): lax.all_to_all(jnp.stack([packet[None]] * lax.axis_size('rows')), 'rows',...]
  transfers between devices with their start and end apart: 6 -> 7, of which waited for: 5 -> 6; matrix products, arithmetic and copies ran while one was open for 0% -> 0% of each run, Pallas kernels for 0% -> 0%
where the time goes in v1:
time: 787 us; the launch traced here: 778 us
  waiting for transfers between devices  506 us (64%)
  local copies, waits for them, and re-layouts  110 us (14%)
  matrix products  75.8 us (10%)
  starting transfers between devices  31.8 us (4%)
  blocking collectives  28.6 us (4%)
  between operations  14.9 us (2%)
  other arithmetic  10.4 us (1%)
    unnamed x3, waiting for transfers between devices  410 us
    all_gather x1, waiting for transfers between devices, body(): lax.all_gather(conv_out, 'ch', axis=1, tiled=True)  56.4 us
    dot_general x14, matrix products, over_second(): return jnp.einsum('...kb,bm->...km', values, matrix, precision=exact)  38.6 us
    dot_general x14, matrix products, over_first(): return jnp.einsum('ka,...ab->...kb', matrix, values, precision=exact)  34.2 us
    all_to_all x1, waiting for transfers between devices, body(): lax.all_to_all(jnp.stack([packet[None]] * lax.axis_size('rows')), 'rows',...  17.8 us
    all_to_all x1, waiting for transfers between devices, body(): lax.all_to_all(wire, 'rows', split_axis=3, concat_axis=1, tiled=True)  17.4 us
    unnamed x37, local copies, waits for them, and re-layouts  17 us
    all_gather x1, blocking collectives, body(): lax.all_gather(jnp.concatenate([key_weight, query_weight], axis=1), 'ch',...  16.9 us
  transfers between devices with their start and end apart: 7, of which 6 were waited for; matrix products, arithmetic and copies ran while one was open for 0% of the time, Pallas kernels for 0%

profile of v1, /device:TPU:32, one launch (start us, length us, event | category | flops | bytes accessed | tf_op | source)
XLA Modules:
  0.0 777.6 jit_solution(9291709852071003650)
XLA Ops:
  17.9 56.4 %all-gather.2.cloned.1.call-done = bf16[4,96,2048]{2,1,0:T(8,128)(2,1)} async-done(((bf16[4,24,2048]{2,1,0:T(8,128)(2,1)}), bf16[4,96,2048]{2,1,0:T(8,128)(2,1)}) %all-gather.2.cloned.1.call-update) | async-done | bytes 1572880 | tf_op jit(solution)/shard_map/all_gather | solution.py:136
  92.5 3.8 fusion.45
  100.3 3.6 reshape.436
  103.8 11.0 %all-to-all-start = ((bf16[64,2,1536]{2,1,0:T(2,128)(2,1)}), bf16[64,2,1536]{2,1,0:T(2,128)(2,1)S(1)}, u32[]{:S(2)}, u32[]{:S(2)}) async-start(bf16[64,2,1536]{2,1,0:T(2,128)(2,1)} %reshape.436), calls=%async_computation | async-start | bytes 786432 | tf_op jit(solution)/shard_map/all_to_all | solution.py:145
  115.1 17.4 %all-to-all-done = bf16[64,2,1536]{2,1,0:T(2,128)(2,1)S(1)} async-done(((bf16[64,2,1536]{2,1,0:T(2,128)(2,1)}), bf16[64,2,1536]{2,1,0:T(2,128)(2,1)S(1)}, u32[]{:S(2)}, u32[]{:S(2)}) %all-to-all-start) | async-done | bytes 393248 | tf_op jit(solution)/shard_map/all_to_all | solution.py:145
  132.4 3.9 reshape.437
  136.4 5.5 copy.281
  144.6 3.6 copy.219
  153.5 4.1 copy.223
  166.8 3.8 subtract_bitcast_fusion
  170.5 4.0 add_bitcast_fusion
  174.5 3.8 copy.236
  180.5 3.8 copy.233
  203.0 3.8 copy.239
  206.9 3.8 convolution_subtract_fusion
  224.5 3.9 copy.247
  237.3 3.6 reshape.438
  240.9 4.8 all-to-all-start.1
  245.7 16.9 %all_gather.11 = bf16[96,256]{1,0:T(8,128)(2,1)S(1)} all-gather(bf16[24,256]{1,0:T(8,128)(2,1)S(1)} %pad_maximum_fusion.4), channel_id=1, replica_groups=mesh['rows'=64,'ch'=4] {'ch'}, dimensions={0}, use_global_device_ids=true | all-gather | bytes 61440 | tf_op jit(solution)/shard_map/all_gather | solution.py:175
  308.1 4.9 gather_fusion
  313.0 11.7 %all_gather.10 = bf16[320,96]{0,1:T(8,128)(2,1)S(1)} all-gather(bf16[320,24]{0,1:T(8,128)(2,1)S(1)} %copy.260), channel_id=1, replica_groups=mesh['rows'=64,'ch'=4] {'ch'}, dimensions={1}, use_global_device_ids=true | all-gather | bytes 76800 | tf_op jit(solution)/shard_map/all_gather | solution.py:180
  326.0 12.8 %all-to-all-start.2 = ((bf16[64,1,17,128]{3,2,1,0:T(8,128)(2,1)}), bf16[64,1,17,128]{3,2,1,0:T(8,128)(2,1)S(1)}, u32[]{:S(2)}, u32[]{:S(2)}) async-start(bf16[64,1,17,128]{3,2,1,0:T(8,128)(2,1)} %stack.29), calls=%async_computation.2 | async-start | bytes 786432 | tf_op jit(solution)/shard_map/all_to_all | solution.py:194
  339.1 17.8 %all-to-all-done.2 = bf16[64,1,17,128]{3,2,1,0:T(8,128)(2,1)S(1)} async-done(((bf16[64,1,17,128]{3,2,1,0:T(8,128)(2,1)}), bf16[64,1,17,128]{3,2,1,0:T(8,128)(2,1)S(1)}, u32[]{:S(2)}, u32[]{:S(2)}) %all-to-all-start.2) | async-done | bytes 278560 | tf_op jit(solution)/shard_map/all_to_all | solution.py:194
  358.7 410.4 %reduce-scatter.4.cloned.1.call-done = f32[16,2]{1,0:T(8,128)} async-done(((f32[1024,2]{1,0:T(8,128)}), f32[16,2]{1,0:T(8,128)}) %reduce-scatter.4.cloned.1.call-update) | async-done | bytes 144
  (134 shorter events, 143.7 us)
Async XLA Ops:
  7.2 67.2 %copy-start = (bf16[96,96]{1,0:T(8,128)(2,1)S(1)}, bf16[96,96]{1,0:T(8,128)(2,1)}, u32[]{:S(2)}) copy-start(bf16[96,96]{1,0:T(8,128)(2,1)} %param.12) | copy-start | bytes 55300
  7.2 8.8 %copy-start.5 = (bf16[4,24,2048]{2,1,0:T(8,128)(2,1)S(1)}, bf16[4,24,2048]{2,1,0:T(8,128)(2,1)}, u32[]{:S(2)}) copy-start(bf16[4,24,2048]{2,1,0:T(8,128)(2,1)} %param.10) | copy-start | bytes 1179652
  7.2 67.1 %all-gather.2.cloned.1.call-start = ((), (), s32[]{:S(2)}) async-start(), calls=%async_computation.4 | async-start | bytes 1966080 | tf_op jit(solution)/shard_map/all_gather | solution.py:136
  8.3 4.0 collective-permute-start
  10.1 4.6 collective-permute-start.1
  76.3 0.8 copy-start.7
  77.9 0.9 copy-start.4
  100.2 14.6 %copy-start.12 = (s32[256]{0:T(256)S(1)}, s32[256]{0:T(256)}, u32[]{:S(2)}) copy-start(s32[256]{0:T(256)} %param.18) | copy-start | bytes 3076
  100.2 14.6 %copy-start.13 = (s32[64]{0:T(128)S(1)}, s32[64]{0:T(128)}, u32[]{:S(2)}) copy-start(s32[64]{0:T(128)} %param.17) | copy-start | bytes 772
  103.8 28.6 %all-to-all-start = ((bf16[64,2,1536]{2,1,0:T(2,128)(2,1)}), bf16[64,2,1536]{2,1,0:T(2,128)(2,1)S(1)}, u32[]{:S(2)}, u32[]{:S(2)}) async-start(bf16[64,2,1536]{2,1,0:T(2,128)(2,1)} %reshape.436), calls=%async_computation | async-start | bytes 786432 | tf_op jit(solution)/shard_map/all_to_all | solution.py:145
  157.5 2.0 copy-start.3
  184.3 2.1 copy-start.9
  206.8 3.8 copy-start.2
  237.2 8.5 %copy-start.10 = (bf16[24,128]{1,0:T(8,128)(2,1)S(1)}, bf16[24,128]{1,0:T(8,128)(2,1)}, u32[]{:S(2)}) copy-start(bf16[24,128]{1,0:T(8,128)(2,1)} %param.15) | copy-start | bytes 18436
  237.2 8.5 %copy-start.11 = (bf16[24,128]{1,0:T(8,128)(2,1)S(1)}, bf16[24,128]{1,0:T(8,128)(2,1)}, u32[]{:S(2)}) copy-start(bf16[24,128]{1,0:T(8,128)(2,1)} %param.16) | copy-start | bytes 18436
  237.3 25.4 %copy-start.14 = (s32[64]{0:T(128)S(1)}, s32[64]{0:T(128)}, u32[]{:S(2)}) copy-start(s32[64]{0:T(128)} %param.19) | copy-start | bytes 772
  240.9 23.6 %all-to-all-start.1 = ((bf16[64,2,1536]{2,1,0:T(2,128)(2,1)}), bf16[64,2,1536]{2,1,0:T(2,128)(2,1)S(1)}, u32[]{:S(2)}, u32[]{:S(2)}) async-start(bf16[64,2,1536]{2,1,0:T(2,128)(2,1)} %reshape.438), calls=%async_computation.1 | async-start | bytes 786432 | tf_op jit(solution)/shard_map/all_to_all | solution.py:158
  287.6 1.5 copy-start.8
  307.0 19.0 %copy-start.6 = (bf16[4,24,2048]{2,1,0:T(8,128)(2,1)}, bf16[4,24,2048]{2,1,0:T(8,128)(2,1)S(1)}, u32[]{:S(2)}) copy-start(bf16[4,24,2048]{2,1,0:T(8,128)(2,1)S(1)} %add_convert_fusion.1) | copy-start | bytes 1179652
  326.0 30.9 %all-to-all-start.2 = ((bf16[64,1,17,128]{3,2,1,0:T(8,128)(2,1)}), bf16[64,1,17,128]{3,2,1,0:T(8,128)(2,1)S(1)}, u32[]{:S(2)}, u32[]{:S(2)}) async-start(bf16[64,1,17,128]{3,2,1,0:T(8,128)(2,1)} %stack.29), calls=%async_computation.2 | async-start | bytes 786432 | tf_op jit(solution)/shard_map/all_to_all | solution.py:194
  338.8 431.8 %copy-start.1 = (bf16[96,96]{1,0:T(8,128)(2,1)S(1)}, bf16[96,96]{1,0:T(8,128)(2,1)}, u32[]{:S(2)}) copy-start(bf16[96,96]{1,0:T(8,128)(2,1)} %param.12) | copy-start | bytes 55300
  338.8 430.3 %reduce-scatter.4.cloned.1.call-start = ((), (), s32[]{:S(2)}) async-start(), calls=%async_computation.5 | async-start | bytes 532480
Sparse Core Ops, SparseCore 0:
  17.9 56.3 all-gather.1
  358.8 410.2 reduce-scatter.3
